TPU v7x, 256 devices: a whole 4x4x8 slice. The times are simulated.
256 devices in a mesh: ctx: 8 (over z_lo, core), ep: 32 (over y, x, z_hi).
Axes of the slice: x: 4, y: 4, z: 8 (z_hi: 2, z_lo: 4; z = z_hi * 4 + z_lo), core: 2. Of those that a mesh axis runs over, the one named last changes fastest.
Arguments:
- queries: bfloat16 [32768, 2048], P(('ctx', 'ep')), may hold values from -40 to 40
- keys: bfloat16 [32768, 256], P(('ctx', 'ep')), may hold values from -40 to 40
- values: bfloat16 [32768, 256], P(('ctx', 'ep')), may hold values from -6 to 6
- prior_out: bfloat16 [32768, 2048], P(('ctx', 'ep')), may hold values from -6 to 6
- prior_lse: float32 [32768, 16], P(('ctx', 'ep')), may hold values from 4 to 8
- residual: bfloat16 [32768, 2048], P(('ctx', 'ep')), may hold values from -40 to 40
- out_proj: bfloat16 [2048, 2048], P(('ctx', 'ep')), may hold values from -0.5 to 0.5
- norm_gain: float32 [2048], replicated, may hold values from 0.5 to 1.5
- expert_in: bfloat16 [32, 2048, 1536], P('ep'), may hold values from -0.125 to 0.125
- expert_out: bfloat16 [32, 768, 2048], P('ep'), may hold values from -0.21875 to 0.21875
- expert_ids: int32 [32768, 8], P(('ctx', 'ep')), may hold values from 0 to 31, as said below
- route_weight: float32 [32768, 8], P(('ctx', 'ep')), may hold values from 0.05 to 0.6
Outputs:
- layer_out: bfloat16 [32768, 2048], P(('ctx', 'ep'))
- attended: bfloat16 [32768, 2048], P(('ctx', 'ep'))
Inputs may be any that keep to these rules, and one draw needn't show every extreme that they name: `expert_ids`: each row names 8 different experts. In the rows of one device no expert is named more than 40 times, and one expert is named exactly 40 times in the rows of every device.
All inputs are finite; a program needn't handle non-finite values.
Results may differ from a plain program's by a relative error of at most 0.0061.
Values may be sent and summed in bfloat16 or wider, within the bound.
A program may use at most 128 MiB of HBM per device.

v0:
```python
import math
import jax
import jax.numpy as jnp
from jax import lax
from jax.sharding import PartitionSpec as P

HEADS = 16
KVH = 2
HD = 128
GROUP = 8


def passed_along(shard, axis, by):
    devices = lax.axis_size(axis)
    return lax.ppermute(shard, axis, [(i, (i + by) % devices) for i in range(devices)])


def run_expert(inputs, weight_in, weight_out, hidden_units):
    flat_in = inputs.reshape(-1, inputs.shape[-1])
    gate_up = jnp.dot(flat_in, weight_in, preferred_element_type=jnp.float32)
    activated = (jax.nn.silu(gate_up[:, :hidden_units]) * gate_up[:, hidden_units:]).astype(
        jnp.bfloat16
    )
    replies = jnp.dot(activated, weight_out, preferred_element_type=jnp.float32).astype(
        jnp.bfloat16
    )
    return replies.reshape(inputs.shape[:-1] + (weight_out.shape[-1],))


def shards(
    queries,
    keys,
    values,
    prior_out,
    prior_lse,
    residual,
    out_proj,
    norm_gain,
    expert_in,
    expert_out,
    expert_ids,
    route_weight,
):
    local_rows = queries.shape[0]
    ctx_count = lax.axis_size("ctx")
    ctx_here = lax.axis_index("ctx")
    ep_count = lax.axis_size("ep")
    reach_steps = min(2, ctx_count - 1)
    kv_pair = jnp.stack([keys, values])
    arrived = []
    current = kv_pair
    for stride in range(reach_steps):
        current = passed_along(current, "ctx", 1)
        arrived.append(current)
    window = jnp.concatenate(arrived, axis=1)
    width_kv = window.shape[1]
    key_win = window[0].reshape(width_kv, KVH, HD)
    value_win = window[1].reshape(width_kv, KVH, HD)
    query_blk = queries.reshape(local_rows, KVH, GROUP, HD)
    scores = jnp.einsum(
        "ighd,jgd->ghij", query_blk, key_win, preferred_element_type=jnp.float32
    ) / math.sqrt(HD)
    positions = jnp.arange(width_kv, dtype=jnp.int32)
    key_local = positions % local_rows
    key_ctx = (ctx_here - (positions // local_rows + 1)) % ctx_count
    query_local = jnp.arange(local_rows, dtype=jnp.int32)[:, None]
    visible = (key_local[None, :] < query_local) | (key_local[None, :] == query_local) & (
        key_ctx[None, :] <= ctx_here
    )
    scores = jnp.where(visible, scores, -jnp.inf)
    lse_prior = prior_lse.reshape(local_rows, KVH, GROUP).transpose(1, 2, 0)
    top_score = jnp.maximum(lse_prior, jnp.max(scores, axis=-1))
    weights = jnp.exp(scores - top_score[..., None])
    prior_weight = jnp.exp(lse_prior - top_score)
    totals = prior_weight + jnp.sum(weights, axis=-1)
    gathered = jnp.einsum(
        "ghij,jgd->ighd",
        weights.astype(jnp.bfloat16),
        value_win,
        preferred_element_type=jnp.float32,
    )
    prior_part = (
        prior_out.reshape(local_rows, KVH, GROUP, HD).astype(jnp.float32)
        * prior_weight.transpose(2, 0, 1)[..., None]
    )
    attended = ((prior_part + gathered) / totals.transpose(2, 0, 1)[..., None]).astype(jnp.bfloat16)
    attended = attended.reshape(local_rows, HEADS * HD)
    model_width = out_proj.shape[1]
    projected = jnp.dot(
        attended,
        lax.all_gather(out_proj, ("ctx", "ep"), axis=0, tiled=True),
        preferred_element_type=jnp.float32,
    )
    mixed_state = (residual.astype(jnp.float32) + projected).astype(jnp.bfloat16)
    state_f = lax.optimization_barrier(mixed_state).astype(jnp.float32)
    normed = (
        state_f * lax.rsqrt(jnp.mean(state_f * state_f, axis=-1, keepdims=True) + 1e-06) * norm_gain
    ).astype(jnp.bfloat16)
    experts_all = ep_count * expert_in.shape[0]
    top_count = expert_ids.shape[1]
    capacity = max(
        local_rows // 4, top_count * ((local_rows + experts_all - 2) // (experts_all - 1))
    )
    flat_ids = expert_ids.reshape(-1)
    one_hot = (flat_ids[:, None] == jnp.arange(experts_all, dtype=jnp.int32)[None, :]).astype(
        jnp.int32
    )
    earlier = jnp.cumsum(one_hot, axis=0) - one_hot
    slot_ids = flat_ids * capacity + jnp.sum(earlier * one_hot, axis=1)
    outgoing = jnp.zeros((experts_all * capacity, model_width), jnp.bfloat16)
    outgoing = (
        outgoing.at[slot_ids]
        .set(jnp.repeat(normed, top_count, axis=0))
        .reshape(experts_all, capacity, model_width)
    )
    weight_in = expert_in[0]
    weight_out = expert_out[0]
    hidden_units = weight_out.shape[0]
    replies = run_expert(
        lax.all_to_all(outgoing, "ep", split_axis=0, concat_axis=0, tiled=True),
        weight_in,
        weight_out,
        hidden_units,
    )
    returned = lax.all_to_all(replies, "ep", split_axis=0, concat_axis=0, tiled=True)
    picked = returned.reshape(experts_all * capacity, model_width)[slot_ids].reshape(
        local_rows, top_count, model_width
    )
    combined = jnp.sum(route_weight[:, :, None] * picked.astype(jnp.float32), axis=1)
    layer_out = (state_f + combined).astype(jnp.bfloat16)
    return (layer_out, attended)


def solution(mesh):
    return jax.shard_map(
        shards,
        mesh=mesh,
        in_specs=(
            P(("ctx", "ep"), None),
            P(("ctx", "ep"), None),
            P(("ctx", "ep"), None),
            P(("ctx", "ep"), None),
            P(("ctx", "ep"), None),
            P(("ctx", "ep"), None),
            P(("ctx", "ep"), None),
            P(),
            P("ep", None, None),
            P("ep", None, None),
            P(("ctx", "ep"), None),
            P(("ctx", "ep"), None),
        ),
        out_specs=(P(("ctx", "ep"), None), P(("ctx", "ep"), None)),
        check_vma=False,
    )
```

profile of v0, /device:TPU:105, one launch (start us, length us, event | category | flops | bytes accessed | tf_op | source)
XLA Modules:
  0.0 1047.9 jit_solution(17184374419318209309)
XLA Ops:
  7.2 0.7 all-gather.2.cloned.1.call-update
  7.9 1.2 copy.21
  9.1 1.0 copy.22
  10.0 0.7 pad_maximum_fusion
  10.7 0.8 copy.28
  11.6 9.0 reduce-window.6
  20.7 0.1 copy.30
  21.0 0.1 fusion.27
  21.3 0.7 broadcast_multiply_fusion
  22.0 0.1 copy.27
  22.4 2.0 copy.38
  24.4 2.3 copy.20
  26.7 1.0 constant_dynamic-update-slice_fusion.1
  27.8 1.6 fusion.39
  29.4 0.3 fusion.12
  29.7 1.3 fusion.16
  31.0 678.4 %all-gather.2.cloned.1.call-done = bf16[2048,2048]{1,0:T(8,128)(2,1)} async-done(((bf16[8,2048]{1,0:T(8,128)(2,1)}), bf16[2048,2048]{1,0:T(8,128)(2,1)}) %all-gather.2.cloned.1.call-update) | async-done | bytes 8388624 | tf_op jit(solution)/shard_map/all_gather | solution.py:91
  709.4 4.9 fusion.8
  714.3 0.2 fusion.17
  714.5 0.6 copy-done.1
  715.1 1.0 fusion.19
  716.1 10.1 scatter_custom_fusion
  726.2 146.0 %all_to_all.10 = bf16[32,40,2048]{2,1,0:T(8,128)(2,1)S(1)} all-to-all(bf16[32,40,2048]{2,1,0:T(8,128)(2,1)} %bitcast.79), channel_id=1, replica_groups=mesh['ctx'=8,'ep'=32] {'ep'}, dimensions={0} | all-to-all | bytes 10485760 | tf_op jit(solution)/shard_map/all_to_all | solution.py:120
  872.2 10.5 %fusion.1 = f32[1280,1536]{1,0:T(8,128)S(1)} fusion(bf16[1280,2048]{1,0:T(8,128)(2,1)S(1)} %bitcast.81, bf16[1,2048,1536]{2,1,0:T(8,128)(2,1)} %param.20), kind=kOutput, calls=%fused_computation.5 | convolution fusion | flops 8053063680 | bytes 19398656 | tf_op jit(solution)/shard_map/dot_general | solution.py:20
  882.7 6.1 convolution_convert_fusion
  888.8 8.2 all-to-all-start.1
  897.0 0.1 copy.26
  897.1 2.0 copy.32
  899.2 122.4 %all-to-all-done.1 = bf16[32,40,2048]{2,1,0:T(8,128)(2,1)} async-done(((bf16[32,40,2048]{2,1,0:T(8,128)(2,1)}), bf16[32,40,2048]{2,1,0:T(8,128)(2,1)}, u32[]{:S(2)}, u32[]{:S(2)}) %all-to-all-start.1) | async-done | bytes 5242912 | tf_op jit(solution)/shard_map/all_to_all | solution.py:125
  1021.6 12.0 %gather_fusion = bf16[1024,2048]{1,0:T(8,128)(2,1)} fusion(bf16[1280,2048]{1,0:T(8,128)(2,1)} %bitcast.25, s32[1024]{0:T(1024)S(1)} %broadcast_clamp_fusion), kind=kCustom, calls=%fused_computation | custom fusion | bytes 8392704 | tf_op jit(solution)/shard_map/gather | solution.py:126
  1033.6 6.6 fusion
  1040.2 0.9 fusion.20
  (37 shorter events, 0.9 us)
Async XLA Ops:
  7.2 875.5 %copy-start = (bf16[1,768,2048]{2,1,0:T(8,128)(2,1)S(1)}, bf16[1,768,2048]{2,1,0:T(8,128)(2,1)}, u32[]{:S(2)}) copy-start(bf16[1,768,2048]{2,1,0:T(8,128)(2,1)} %param.21) | copy-start | bytes 9437188
  7.2 702.3 %all-gather.2.cloned.1.call-start = ((), (), s32[]{:S(2)}) async-start(), calls=%async_computation.2 | async-start | bytes 8421376 | tf_op jit(solution)/shard_map/all_gather | solution.py:91
  10.0 19.3 %copy-start.4 = (f32[128,16]{0,1:T(8,128)S(1)}, f32[128,16]{0,1:T(8,128)}, u32[]{:S(2)}) copy-start(f32[128,16]{0,1:T(8,128)} %param.16) | copy-start | bytes 24580
  10.7 11.6 %collective-permute-start = (bf16[2,128,256]{1,2,0:T(8,128)(2,1)}, bf16[2,128,256]{1,2,0:T(8,128)(2,1)}, u32[]{:S(2)}, u32[]{:S(2)}) collective-permute-start(bf16[2,128,256]{1,2,0:T(8,128)(2,1)} %pad_maximum_fusion), channel_id=1, source_target_pairs={{0,32},{32,64},{64,96},{96,128},{128,160},{160,192},{192,224},{224... | collective-permute-start | bytes 393224 | tf_op jit(solution)/shard_map/ppermute | solution.py:15
  22.3 5.4 collective-permute-start.1
  26.7 3.0 copy-start.3
  709.4 5.7 copy-start.5
  714.3 0.8 copy-start.1
  888.8 8.2 copy-start.6
  888.8 132.7 %all-to-all-start.1 = ((bf16[32,40,2048]{2,1,0:T(8,128)(2,1)}), bf16[32,40,2048]{2,1,0:T(8,128)(2,1)}, u32[]{:S(2)}, u32[]{:S(2)}) async-start(bf16[32,40,2048]{2,1,0:T(8,128)(2,1)} %bitcast.80), calls=%async_computation.1 | async-start | bytes 10485760 | tf_op jit(solution)/shard_map/all_to_all | solution.py:125
  1033.6 6.6 copy-start.2
Sparse Core Ops, SparseCore 0:
  9.9 699.5 all-gather.1
where the time goes:
time: 1050 us
  waiting for transfers between devices  801 us (76%)
  blocking collectives  146 us (14%)
  local copies, waits for them, and re-layouts  33.8 us (3%)
  matrix products  24.4 us (2%)
  other arithmetic  19.7 us (2%)
  between operations  14.3 us (1%)
    all_gather x1, waiting for transfers between devices, shards(): lax.all_gather(out_proj, ('ctx', 'ep'), axis=0, tiled=True)  678 us
    all_to_all x1, blocking collectives, shards(): lax.all_to_all(outgoing, 'ep', split_axis=0, concat_axis=0, tiled=True)  146 us
    all_to_all x1, waiting for transfers between devices, shards(): lax.all_to_all(replies, 'ep', split_axis=0, concat_axis=0, tiled=True)  122 us
  transfers between devices with their start and end apart: 4, of which 2 were waited for; matrix products, arithmetic and copies ran while one was open for 2% of the time, Pallas kernels for 0%

commit v1 on v0

--- a/solution.py
+++ b/solution.py
@@ -86,10 +86,15 @@
     attended = ((prior_part + gathered) / totals.transpose(2, 0, 1)[..., None]).astype(jnp.bfloat16)
     attended = attended.reshape(local_rows, HEADS * HD)
     model_width = out_proj.shape[1]
+
+    def register_sums_all_over_axis(row_data):
+        d_next = jax.lax.axis_size(("ctx", "ep"))
+        later = jnp.stack(d_next * [row_data])
+        mat_out = jax.lax.all_to_all(later, ("ctx", "ep"), 0, 0)
+        return jnp.concatenate(mat_out, axis=0)
+
     projected = jnp.dot(
-        attended,
-        lax.all_gather(out_proj, ("ctx", "ep"), axis=0, tiled=True),
-        preferred_element_type=jnp.float32,
+        attended, register_sums_all_over_axis(out_proj), preferred_element_type=jnp.float32
     )
     mixed_state = (residual.astype(jnp.float32) + projected).astype(jnp.bfloat16)
     state_f = lax.optimization_barrier(mixed_state).astype(jnp.float32)

time: 1050 us -> 533 us (0.51)
  waiting for transfers between devices: 801 us -> 293 us
  starting transfers between devices: 8.32 us -> 26.3 us
  blocking collectives: 146 us -> 132 us
  between operations: 14.3 us -> 0.9 us
    all_gather x1 -> x0, waiting for transfers between devices: 678 us -> none  [shards(): lax.all_gather(out_proj, ('ctx', 'ep'), axis=0, tiled=True)]
    ppermute x2, waiting for transfers between devices: 0.01 us -> 166 us  [passed_along(): lax.ppermute(shard, axis, [(i, (i + by) % devices) for i in range(devices)])]
    all_to_all x0 -> x1, starting transfers between devices: none -> 15.3 us  [register_sums_all_over_axis(): mat_out = jax.lax.all_to_all(later, ('ctx', 'ep'), 0, 0)]
    all_to_all x1, blocking collectives: 146 us -> 132 us  [shards(): lax.all_to_all(outgoing, 'ep', split_axis=0, concat_axis=0, tiled=True)]
  transfers between devices with their start and end apart: 4 -> 4, of which waited for: 2 -> 2; matrix products, arithmetic and copies ran while one was open for 2% -> 4% of each run, Pallas kernels for 0% -> 0%
where the time goes in v1:
time: 533 us; the launch traced here: 532 us
  waiting for transfers between devices  293 us (55%)
  blocking collectives  132 us (25%)
  local copies, waits for them, and re-layouts  36.4 us (7%)
  starting transfers between devices  26.3 us (5%)
  matrix products  24.4 us (5%)
  other arithmetic  19 us (4%)
    ppermute x2, waiting for transfers between devices, passed_along(): lax.ppermute(shard, axis, [(i, (i + by) % devices) for i in range(devices)])  166 us
    all_to_all x1, blocking collectives, shards(): lax.all_to_all(outgoing, 'ep', split_axis=0, concat_axis=0, tiled=True)  132 us
    all_to_all x1, waiting for transfers between devices, shards(): lax.all_to_all(replies, 'ep', split_axis=0, concat_axis=0, tiled=True)  126 us
    all_to_all x1, starting transfers between devices, register_sums_all_over_axis(): mat_out = jax.lax.all_to_all(later, ('ctx', 'ep'), 0, 0)  15.3 us
    gather x1, local copies, waits for them, and re-layouts, shards(): returned.reshape(experts_all * capacity, model_width)[slot_ids]  12 us
  transfers between devices with their start and end apart: 4, of which 2 were waited for; matrix products, arithmetic and copies ran while one was open for 4% of the time, Pallas kernels for 0%

profile of v1, /device:TPU:105, one launch (start us, length us, event | category | flops | bytes accessed | tf_op | source)
XLA Modules:
  0.0 531.7 jit_solution(3390048454638357686)
XLA Ops:
  0.6 5.2 stack.11
  5.8 15.3 %all-to-all-start = ((bf16[256,8,2048]{2,1,0:T(8,128)(2,1)}), bf16[256,8,2048]{2,1,0:T(8,128)(2,1)}, u32[]{:S(2)}, u32[]{:S(2)}) async-start(bf16[256,8,2048]{2,1,0:T(8,128)(2,1)} %stack.11), calls=%async_computation | async-start | bytes 16777216 | tf_op jit(solution)/shard_map/all_to_all | solution.py:93
  21.1 0.1 copy.21
  21.3 0.1 copy.22
  21.4 0.7 pad_maximum_fusion
  22.3 9.0 %reduce-window.6 = s32[32,8,128]{2,1,0:T(8,128)S(1)} reduce-window(s32[32,8,128]{2,1,0:T(8,128)S(1)} %fusion.36, s32[]{:T(128)} %constant.58.clone.1), window={size=1x1x128 pad=0_0x0_0x127_0}, to_apply=%region_2.3 | reduce-window | flops 4161536 | bytes 262148 | tf_op jit(solution)/shard_map/reduce-window
  31.4 0.1 copy.30
  31.7 0.1 fusion.34
  32.0 0.1 copy.27
  32.3 166.3 %collective-permute-done = bf16[2,128,256]{1,2,0:T(8,128)(2,1)} collective-permute-done((bf16[2,128,256]{1,2,0:T(8,128)(2,1)}, bf16[2,128,256]{1,2,0:T(8,128)(2,1)}, u32[]{:S(2)}, u32[]{:S(2)}) %collective-permute-start) | collective-permute-done | bytes 131104 | tf_op jit(solution)/shard_map/ppermute | solution.py:15
  198.6 4.3 collective-permute-start.1
  202.9 2.0 copy.38
  204.8 2.2 copy.20
  207.1 1.0 constant_dynamic-update-slice_fusion.1
  208.2 1.6 fusion.46
  209.8 0.3 fusion.19
  210.1 1.3 fusion.23
  211.4 4.9 fusion.13
  216.3 0.2 fusion.24
  216.5 0.6 copy-done.1
  217.1 1.0 fusion.26
  218.1 10.1 %scatter_custom_fusion = bf16[1280,2048]{1,0:T(8,128)(2,1)} fusion(s32[1024]{0:T(1024)S(1)} %bitcast.100, bf16[]{:T(256)} %constant.69.clone.1, bf16[128,2048]{1,0:T(8,128)(2,1)} %fusion.26), kind=kCustom, calls=%fused_computation.9 | custom fusion | bytes 5767170 | tf_op jit(solution)/shard_map/scatter | solution.py:118
  228.2 132.1 %all_to_all.15 = bf16[32,40,2048]{2,1,0:T(8,128)(2,1)S(1)} all-to-all(bf16[32,40,2048]{2,1,0:T(8,128)(2,1)} %bitcast.85), channel_id=1, replica_groups=mesh['ctx'=8,'ep'=32] {'ep'}, dimensions={0} | all-to-all | bytes 10485760 | tf_op jit(solution)/shard_map/all_to_all | solution.py:125
  360.3 10.5 %fusion.3 = f32[1280,1536]{1,0:T(8,128)S(1)} fusion(bf16[1280,2048]{1,0:T(8,128)(2,1)S(1)} %bitcast.87, bf16[1,2048,1536]{2,1,0:T(8,128)(2,1)} %param.20), kind=kOutput, calls=%fused_computation.7 | convolution fusion | flops 8053063680 | bytes 19398656 | tf_op jit(solution)/shard_map/dot_general | solution.py:20
  370.8 6.1 %convolution_convert_fusion = bf16[1280,2048]{1,0:T(8,128)(2,1)} fusion(bf16[1,768,2048]{2,1,0:T(8,128)(2,1)S(1)} %copy-done, f32[1280,1536]{1,0:T(8,128)S(1)} %fusion.3), kind=kOutput, calls=%fused_computation.6 | convolution fusion | flops 4035051520 | bytes 16252928 | tf_op jit(solution)/shard_map/dot_general | solution.py:24
  376.9 6.7 %all-to-all-start.2 = ((bf16[32,40,2048]{2,1,0:T(8,128)(2,1)}), bf16[32,40,2048]{2,1,0:T(8,128)(2,1)}, u32[]{:S(2)}, u32[]{:S(2)}) async-start(bf16[32,40,2048]{2,1,0:T(8,128)(2,1)} %bitcast.86), calls=%async_computation.2 | async-start | bytes 10485760 | tf_op jit(solution)/shard_map/all_to_all | solution.py:130
  383.6 0.1 copy.26
  383.7 2.0 copy.32
  385.8 126.4 %all-to-all-done.2 = bf16[32,40,2048]{2,1,0:T(8,128)(2,1)} async-done(((bf16[32,40,2048]{2,1,0:T(8,128)(2,1)}), bf16[32,40,2048]{2,1,0:T(8,128)(2,1)}, u32[]{:S(2)}, u32[]{:S(2)}) %all-to-all-start.2) | async-done | bytes 5242912 | tf_op jit(solution)/shard_map/all_to_all | solution.py:130
  512.2 12.0 %gather_fusion = bf16[1024,2048]{1,0:T(8,128)(2,1)} fusion(bf16[1280,2048]{1,0:T(8,128)(2,1)} %bitcast.26, s32[1024]{0:T(1024)S(1)} %broadcast_clamp_fusion), kind=kCustom, calls=%fused_computation | custom fusion | bytes 8392704 | tf_op jit(solution)/shard_map/gather | solution.py:131
  524.2 6.6 %fusion = f32[128,2048]{1,0:T(8,128)S(1)} fusion(bf16[1024,2048]{1,0:T(8,128)(2,1)} %gather_fusion, f32[128,8]{1,0:T(8,128)S(1)} %copy.26), kind=kLoop, calls=%fused_computation.3 | loop fusion | flops 6029312 | bytes 5246976 | tf_op jit(solution)/shard_map/reduce_sum | solution.py:134
  530.8 0.9 fusion.27
  (43 shorter events, 0.9 us)
Async XLA Ops:
  0.6 370.2 %copy-start = (bf16[1,768,2048]{2,1,0:T(8,128)(2,1)S(1)}, bf16[1,768,2048]{2,1,0:T(8,128)(2,1)}, u32[]{:S(2)}) copy-start(bf16[1,768,2048]{2,1,0:T(8,128)(2,1)} %param.21) | copy-start | bytes 9437188
  5.8 15.3 %copy-start.4 = (bf16[128,256]{1,0:T(8,128)(2,1)S(1)}, bf16[128,256]{1,0:T(8,128)(2,1)}, u32[]{:S(2)}) copy-start(bf16[128,256]{1,0:T(8,128)(2,1)} %param.13) | copy-start | bytes 196612
  5.8 15.4 %copy-start.5 = (bf16[128,256]{1,0:T(8,128)(2,1)S(1)}, bf16[128,256]{1,0:T(8,128)(2,1)}, u32[]{:S(2)}) copy-start(bf16[128,256]{1,0:T(8,128)(2,1)} %param.14) | copy-start | bytes 196612
  5.8 16.2 %copy-start.7 = (s32[128,8]{0,1:T(8,128)S(1)}, s32[128,8]{0,1:T(8,128)}, u32[]{:S(2)}) copy-start(s32[128,8]{0,1:T(8,128)} %param.22) | copy-start | bytes 12292
  5.8 205.6 %all-to-all-start = ((bf16[256,8,2048]{2,1,0:T(8,128)(2,1)}), bf16[256,8,2048]{2,1,0:T(8,128)(2,1)}, u32[]{:S(2)}, u32[]{:S(2)}) async-start(bf16[256,8,2048]{2,1,0:T(8,128)(2,1)} %stack.11), calls=%async_computation | async-start | bytes 16777216 | tf_op jit(solution)/shard_map/all_to_all | solution.py:93
  21.4 188.4 %copy-start.6 = (f32[128,16]{0,1:T(8,128)S(1)}, f32[128,16]{0,1:T(8,128)}, u32[]{:S(2)}) copy-start(f32[128,16]{0,1:T(8,128)} %param.16) | copy-start | bytes 24580
  22.1 176.5 %collective-permute-start = (bf16[2,128,256]{1,2,0:T(8,128)(2,1)}, bf16[2,128,256]{1,2,0:T(8,128)(2,1)}, u32[]{:S(2)}, u32[]{:S(2)}) collective-permute-start(bf16[2,128,256]{1,2,0:T(8,128)(2,1)} %pad_maximum_fusion), channel_id=1, source_target_pairs={{0,32},{32,64},{64,96},{96,128},{128,160},{160,192},{192,224},{224... | collective-permute-start | bytes 393224 | tf_op jit(solution)/shard_map/ppermute | solution.py:15
  198.6 9.5 %collective-permute-start.1 = (bf16[2,128,256]{1,2,0:T(8,128)(2,1)}, bf16[2,128,256]{1,2,0:T(8,128)(2,1)S(1)}, u32[]{:S(2)}, u32[]{:S(2)}) collective-permute-start(bf16[2,128,256]{1,2,0:T(8,128)(2,1)} %collective-permute-done), channel_id=1, source_target_pairs={{0,32},{32,64},{64,96},{96,128},{128,160},{160,192},{192,224},{224... | collective-permute-start | bytes 393224 | tf_op jit(solution)/shard_map/ppermute | solution.py:15
  207.1 3.0 copy-start.3
  211.4 5.7 %copy-start.8 = (f32[2048]{0:T(1024)S(1)}, f32[2048]{0:T(1024)}, u32[]{:S(2)}) copy-start(f32[2048]{0:T(1024)} %param.19) | copy-start | bytes 24580
  216.3 0.8 copy-start.1
  376.9 6.7 %copy-start.9 = (f32[128,8]{0,1:T(8,128)S(1)}, f32[128,8]{0,1:T(8,128)}, u32[]{:S(2)}) copy-start(f32[128,8]{0,1:T(8,128)} %param.23) | copy-start | bytes 12292
  376.9 135.3 %all-to-all-start.2 = ((bf16[32,40,2048]{2,1,0:T(8,128)(2,1)}), bf16[32,40,2048]{2,1,0:T(8,128)(2,1)}, u32[]{:S(2)}, u32[]{:S(2)}) async-start(bf16[32,40,2048]{2,1,0:T(8,128)(2,1)} %bitcast.86), calls=%async_computation.2 | async-start | bytes 10485760 | tf_op jit(solution)/shard_map/all_to_all | solution.py:130
  524.2 6.6 %copy-start.2 = (bf16[128,2048]{1,0:T(8,128)(2,1)S(1)}, bf16[128,2048]{1,0:T(8,128)(2,1)}, u32[]{:S(2)}) copy-start(bf16[128,2048]{1,0:T(8,128)(2,1)} %copy-done.1) | copy-start | bytes 1572868
